TPU v7x, 256 devices: a whole 4x4x8 slice. The times are simulated.
256 devices in a mesh: section: 8 (over y, core), expert: 32 (over x, z).
Axes of the slice: x: 4, y: 4, z: 8, core: 2. Of those that a mesh axis runs over, the one named last changes fastest.
Arguments:
- handoff: bfloat16 [8, 4096, 2048], P('section', 'expert'), may hold values from -6 to 6
- cotangent_handoff: bfloat16 [8, 4096, 2048], P('section', 'expert'), may hold values from -6 to 6
- saved_input: bfloat16 [8, 4096, 2048], P('section', 'expert'), may hold values from -6 to 6
- norm_gain: float32 [8, 2048], P('section'), may hold values from 0.1 to 1.9
- w_gate: bfloat16 [8, 32, 2048, 768], P('section', 'expert'), may hold values from -0.125 to 0.125
- w_up: bfloat16 [8, 32, 2048, 768], P('section', 'expert'), may hold values from -0.125 to 0.125
- w_down: bfloat16 [8, 32, 768, 2048], P('section', 'expert'), may hold values from -1.25 to 1.25
- picks_fwd: int32 [8, 4096, 8], P('section', 'expert'), may hold values from 0 to 127, as said below
- picks_bwd: int32 [8, 4096, 8], P('section', 'expert'), may hold values from 0 to 127, as said below
- gates_fwd: float32 [8, 4096, 8], P('section', 'expert'), may hold values from 0.05 to 1
- gates_bwd: float32 [8, 4096, 8], P('section', 'expert'), may hold values from 0.05 to 1
Outputs:
- act_out: bfloat16 [8, 4096, 2048], P('section', 'expert')
- grad_out: bfloat16 [8, 4096, 2048], P('section', 'expert')
Inputs may be any that keep to these rules, and one draw needn't show every extreme that they name: `picks_fwd`: each row names 8 different experts. Among the 128 tokens of one section that one expert device holds, no expert is named more than 16 times, and one expert with id below 32 is named exactly 16 times among the tokens of every such device. `picks_bwd`: each row names 8 different experts. Among the 128 tokens of one section that one expert device holds, no expert is named more than 16 times, and one expert with id below 32 is named exactly 16 times among the tokens of every such device.
All inputs are finite; a program needn't handle non-finite values.
Results may differ from a plain program's by a relative error of at most 0.0064.
Values may be sent and summed in bfloat16 or wider, within the bound.
A program may use at most 128 MiB of HBM per device.

v0:
```python
import jax
import jax.numpy as jnp
from jax import lax
from jax.sharding import PartitionSpec as P

NUM_ALL = 128


EPS = 1e-06


def passed_along(value, axis, by):
    peers = lax.axis_size(axis)
    return lax.ppermute(value, axis, [(i, (i + by) % peers) for i in range(peers)])


def normalize(rows, gain):
    values = rows.astype(jnp.float32)
    scale = lax.rsqrt(jnp.mean(values * values, axis=-1) + EPS)
    return ((values * scale[:, None] * gain[None, :]).astype(jnp.bfloat16), scale)


def transposed(left, right):
    return lax.dot_general(
        left, right, (((1,), (1,)), ((), ())), preferred_element_type=jnp.float32
    )


def expert_forward(rows, w_g, w_u, w_d):
    gate_act = jnp.dot(rows, w_g, preferred_element_type=jnp.float32)
    up_act = jnp.dot(rows, w_u, preferred_element_type=jnp.float32)
    hidden = (jax.nn.silu(gate_act) * up_act).astype(jnp.bfloat16)
    return jnp.dot(hidden, w_d, preferred_element_type=jnp.float32).astype(jnp.bfloat16)


def expert_backward(rows, scaled_cot, w_g, w_u, w_d):
    gate_act = jnp.dot(rows, w_g, preferred_element_type=jnp.float32)
    up_act = jnp.dot(rows, w_u, preferred_element_type=jnp.float32)
    sigma = jax.nn.sigmoid(gate_act)
    hid_grad = transposed(scaled_cot, w_d)
    gate_grad = (hid_grad * up_act * sigma * (1.0 + gate_act * (1.0 - sigma))).astype(jnp.bfloat16)
    up_grad = (hid_grad * gate_act * sigma).astype(jnp.bfloat16)
    return (transposed(gate_grad, w_g) + transposed(up_grad, w_u)).astype(jnp.bfloat16)


def route_slots(picks, gates, peers, capacity):
    weight = gates / jnp.sum(gates, axis=1, keepdims=True)
    named = (picks[:, :, None] == jnp.arange(peers, dtype=jnp.int32)[None, None, :]).astype(
        jnp.int32
    )
    per_token = jnp.sum(named, axis=1)
    before = jnp.cumsum(per_token, axis=0) - per_token
    place = jnp.sum(named * before[:, None, :], axis=2)
    slot = jnp.where(picks < peers, picks * capacity + place, peers * capacity)
    return (slot, weight)


def slot_sources(slot, weight, total):
    match = slot[:, :, None] == jnp.arange(total, dtype=jnp.int32)[None, None, :]
    tokens = jnp.arange(slot.shape[0], dtype=jnp.int32)
    source = jnp.sum(jnp.where(match, tokens[:, None, None], 0), axis=(0, 1))
    share = jnp.sum(jnp.where(match, weight[:, :, None], jnp.float32(0.0)), axis=(0, 1))
    filled = jnp.any(match, axis=(0, 1))
    return (source, share, filled)


def gather_back(values, slot, total):
    flat = values.reshape(total, values.shape[-1])
    padded = jnp.concatenate([flat, jnp.zeros((1, flat.shape[1]), flat.dtype)], axis=0)
    return padded[slot]


def local(
    handoff,
    cotangent_handoff,
    saved_input,
    norm_gain,
    w_gate,
    w_up,
    w_down,
    picks_fwd,
    picks_bwd,
    gates_fwd,
    gates_bwd,
):
    arriving = passed_along(handoff, "section", 1)[0]
    upstream = passed_along(cotangent_handoff, "section", -1)[0]
    gain = norm_gain[0]
    w_g = w_gate[0, 0]
    w_u = w_up[0, 0]
    w_d = w_down[0, 0]
    peers = lax.axis_size("expert")
    tok_rows = picks_fwd.shape[1]
    picks_each = picks_fwd.shape[2]
    width = arriving.shape[1]
    capacity = 2 * tok_rows * picks_each // NUM_ALL
    total = peers * capacity
    fwd_normed, unused_scale = normalize(arriving, gain)
    bwd_normed, bwd_scale = normalize(saved_input[0], gain)
    slot_f, weight_f = route_slots(picks_fwd[0], gates_fwd[0], peers, capacity)
    slot_b, weight_b = route_slots(picks_bwd[0], gates_bwd[0], peers, capacity)
    source_f, unused_share, filled_f = slot_sources(slot_f, weight_f, total)
    source_b, share_b, filled_b = slot_sources(slot_b, weight_b, total)
    zero_rows = jnp.zeros((total, width), jnp.bfloat16)
    send_fwd = jnp.where(filled_f[:, None], fwd_normed[source_f], zero_rows).reshape(
        peers, capacity, width
    )
    send_rows = jnp.where(filled_b[:, None], bwd_normed[source_b], zero_rows).reshape(
        peers, capacity, width
    )
    send_cot = (share_b[:, None] * upstream[source_b].astype(jnp.float32)).astype(jnp.bfloat16)
    send_cot = send_cot.reshape(peers, capacity, width)
    fwd_part = lax.all_to_all(send_fwd, "expert", split_axis=0, concat_axis=0, tiled=True)
    row_part = lax.all_to_all(send_rows, "expert", split_axis=0, concat_axis=0, tiled=True)
    cot_part = lax.all_to_all(send_cot, "expert", split_axis=0, concat_axis=0, tiled=True)
    shape = fwd_part.shape
    outputs = expert_forward(fwd_part.reshape(-1, width), w_g, w_u, w_d).reshape(shape)
    grads = expert_backward(
        row_part.reshape(-1, width), cot_part.reshape(-1, width), w_g, w_u, w_d
    ).reshape(shape)
    expert_outs = lax.all_to_all(outputs, "expert", split_axis=0, concat_axis=0, tiled=True)
    expert_grads = lax.all_to_all(grads, "expert", split_axis=0, concat_axis=0, tiled=True)
    picked = gather_back(expert_outs, slot_f, total).astype(jnp.float32)
    mixed = jnp.sum(weight_f[:, :, None] * picked, axis=1)
    act = (arriving.astype(jnp.float32) + mixed).astype(jnp.bfloat16)
    normed_grad = jnp.sum(gather_back(expert_grads, slot_b, total).astype(jnp.float32), axis=1)
    values = saved_input[0].astype(jnp.float32)
    gained = gain[None, :] * normed_grad
    cube = bwd_scale * bwd_scale * bwd_scale
    grad = (
        upstream.astype(jnp.float32)
        + bwd_scale[:, None] * gained
        - values * cube[:, None] * jnp.mean(values * gained, axis=1, keepdims=True)
    ).astype(jnp.bfloat16)
    return (act[None], grad[None])


def solution(mesh):
    in_specs = (
        P("section", "expert", None),
        P("section", "expert", None),
        P("section", "expert", None),
        P("section", None),
        P("section", "expert", None, None),
        P("section", "expert", None, None),
        P("section", "expert", None, None),
        P("section", "expert", None),
        P("section", "expert", None),
        P("section", "expert", None),
        P("section", "expert", None),
    )
    out_specs = (P("section", "expert", None), P("section", "expert", None))
    return jax.shard_map(local, mesh=mesh, in_specs=in_specs, out_specs=out_specs, check_vma=False)
```

profile of v0, /device:TPU:8, one launch (start us, length us, event | category | flops | bytes accessed | tf_op | source)
XLA Modules:
  0.0 387.9 jit_solution(3152473701526599029)
XLA Ops:
  5.4 2.0 fusion.40
  7.4 6.3 %gather_fusion.3 = bf16[512,2048]{1,0:T(8,128)(2,1)} fusion(bf16[128,2048]{1,0:T(8,128)(2,1)} %fusion.40, s32[1024]{0:T(1024)S(1)} %pad_clamp_fusion), kind=kCustom, calls=%fused_computation.3 | custom fusion | bytes 4196352 | tf_op jit(solution)/shard_map/gather | solution.py:108
  13.8 3.2 broadcast_select_fusion
  16.9 11.6 %all-to-all-start.3 = ((bf16[32,16,2048]{2,1,0:T(8,128)(2,1)}), bf16[32,16,2048]{2,1,0:T(8,128)(2,1)}, u32[]{:S(2)}, u32[]{:S(2)}) async-start(bf16[32,16,2048]{2,1,0:T(8,128)(2,1)} %broadcast_select_fusion), calls=%async_computation.3 | async-start | bytes 4194304 | tf_op jit(solution)/shard_map/all_to_all | solution.py:114
  29.1 6.4 %collective-permute-done.1 = bf16[1,128,2048]{2,1,0:T(8,128)(2,1)} collective-permute-done((bf16[1,128,2048]{2,1,0:T(8,128)(2,1)}, bf16[1,128,2048]{2,1,0:T(8,128)(2,1)}, u32[]{:S(2)}, u32[]{:S(2)}) %collective-permute-start.1) | collective-permute-done | bytes 524320 | tf_op jit(solution)/shard_map/ppermute | solution.py:14
  35.5 6.3 %gather_fusion.2 = bf16[512,2048]{1,0:T(8,128)(2,1)} fusion(bf16[128,2048]{1,0:T(8,128)(2,1)} %bitcast.21, s32[1024]{0:T(1024)S(1)} %pad_clamp_fusion), kind=kCustom, calls=%fused_computation.2 | custom fusion | bytes 4196352 | tf_op jit(solution)/shard_map/gather | solution.py:111
  41.9 3.3 fusion.1
  45.2 33.4 %all-to-all-done.3 = bf16[32,16,2048]{2,1,0:T(8,128)(2,1)} async-done(((bf16[32,16,2048]{2,1,0:T(8,128)(2,1)}), bf16[32,16,2048]{2,1,0:T(8,128)(2,1)}, u32[]{:S(2)}, u32[]{:S(2)}) %all-to-all-start.3) | async-done | bytes 2097184 | tf_op jit(solution)/shard_map/all_to_all | solution.py:114
  78.5 6.4 %all-to-all-start.2 = ((bf16[32,16,2048]{2,1,0:T(8,128)(2,1)}), bf16[32,16,2048]{2,1,0:T(8,128)(2,1)}, u32[]{:S(2)}, u32[]{:S(2)}) async-start(bf16[32,16,2048]{2,1,0:T(8,128)(2,1)} %fusion.1), calls=%async_computation.2 | async-start | bytes 4194304 | tf_op jit(solution)/shard_map/all_to_all | solution.py:115
  85.0 5.5 %fusion.14 = f32[512,768]{1,0:T(8,128)} fusion(bf16[512,2048]{1,0:T(8,128)(2,1)} %bitcast.27, bf16[1,1,2048,768]{3,2,1,0:T(8,128)(2,1)} %param.15), kind=kOutput, calls=%fused_computation.23 | convolution fusion | flops 1610612736 | bytes 6815744 | tf_op jit(solution)/shard_map/dot_general | solution.py:37
  90.5 44.0 %all-to-all-done.2 = bf16[32,16,2048]{2,1,0:T(8,128)(2,1)} async-done(((bf16[32,16,2048]{2,1,0:T(8,128)(2,1)}), bf16[32,16,2048]{2,1,0:T(8,128)(2,1)}, u32[]{:S(2)}, u32[]{:S(2)}) %all-to-all-start.2) | async-done | bytes 2097184 | tf_op jit(solution)/shard_map/all_to_all | solution.py:115
  134.5 4.5 %fusion.2 = f32[512,768]{1,0:T(8,128)S(1)} fusion(bf16[512,2048]{1,0:T(8,128)(2,1)} %bitcast.25, bf16[1,1,768,2048]{3,2,1,0:T(8,128)(2,1)} %param.17), kind=kOutput, calls=%fused_computation.11 | convolution fusion | flops 1610612736 | bytes 6815744 | tf_op jit(solution)/shard_map/dot_general | solution.py:24
  140.2 3.8 fusion.6
  143.9 10.0 %add_convert_fusion = bf16[512,2048]{1,0:T(8,128)(2,1)} fusion(f32[512,2048]{1,0:T(8,128)} %fusion.6, bf16[1,1,2048,768]{3,2,1,0:T(8,128)(2,1)} %param.15, f32[512,768]{1,0:T(8,128)} %fusion.14, f32[512,768]{1,0:T(8,128)} %copy-done.13, bf16[512,2048]{1,0:T(8,128)(2,1)} %bitcast.27, bf16[1,1,2048,768]{3,2,1,0:T(8,128)(2,1)S(1)} %copy-done), kind=kOutput, calls=%fused_computation.10 | convolution fusion | flops 3227254784 | bytes 17825792 | tf_op jit(solution)/shard_map/dot_general | solution.py:24
  153.9 6.6 %all-to-all-start.4 = ((bf16[32,16,2048]{2,1,0:T(8,128)(2,1)}), bf16[32,16,2048]{2,1,0:T(8,128)(2,1)}, u32[]{:S(2)}, u32[]{:S(2)}) async-start(bf16[32,16,2048]{2,1,0:T(8,128)(2,1)} %bitcast.132), calls=%async_computation.4 | async-start | bytes 4194304 | tf_op jit(solution)/shard_map/all_to_all | solution.py:122
  162.1 7.4 %collective-permute-done = bf16[1,128,2048]{2,1,0:T(8,128)(2,1)} collective-permute-done((bf16[1,128,2048]{2,1,0:T(8,128)(2,1)}, bf16[1,128,2048]{2,1,0:T(8,128)(2,1)}, u32[]{:S(2)}, u32[]{:S(2)}) %collective-permute-start) | collective-permute-done | bytes 524320 | tf_op jit(solution)/shard_map/ppermute | solution.py:14
  170.7 39.3 %all-to-all-done.4 = bf16[32,16,2048]{2,1,0:T(8,128)(2,1)} async-done(((bf16[32,16,2048]{2,1,0:T(8,128)(2,1)}), bf16[32,16,2048]{2,1,0:T(8,128)(2,1)}, u32[]{:S(2)}, u32[]{:S(2)}) %all-to-all-start.4) | async-done | bytes 2097184 | tf_op jit(solution)/shard_map/all_to_all | solution.py:122
  210.0 3.2 concatenate.7
  213.2 10.7 %gather_fusion.4 = bf16[1024,2048]{1,0:T(8,128)(2,1)} fusion(bf16[513,2048]{1,0:T(8,128)(2,1)} %concatenate.7, s32[1024]{0:T(1024)S(1)} %broadcast_clamp_fusion), kind=kCustom, calls=%fused_computation.4 | custom fusion | bytes 8392704 | tf_op jit(solution)/shard_map/gather | solution.py:70
  223.9 5.1 %convert_reduce_fusion = f32[128,2048]{1,0:T(8,128)S(1)} fusion(bf16[1024,2048]{1,0:T(8,128)(2,1)} %gather_fusion.4), kind=kLoop, calls=%fused_computation.5 | loop fusion | flops 3932160 | bytes 5242880 | tf_op jit(solution)/shard_map/reduce_sum | solution.py:126
  230.0 2.1 fusion.41
  232.1 6.4 %gather_fusion = bf16[512,2048]{1,0:T(8,128)(2,1)} fusion(bf16[128,2048]{1,0:T(8,128)(2,1)} %get-tuple-element.3, s32[1024]{0:T(1024)S(1)} %pad_clamp_fusion.1), kind=kCustom, calls=%fused_computation | custom fusion | bytes 4196352 | tf_op jit(solution)/shard_map/gather | solution.py:105
  238.5 1.8 broadcast_select_fusion.1
  240.3 57.0 %all_to_all.25 = bf16[32,16,2048]{2,1,0:T(8,128)(2,1)S(1)} all-to-all(bf16[32,16,2048]{2,1,0:T(8,128)(2,1)S(1)} %broadcast_select_fusion.1), channel_id=1, replica_groups=mesh['section'=8,'expert'=32] {'expert'}, dimensions={0} | all-to-all | bytes 4194304 | tf_op jit(solution)/shard_map/all_to_all | solution.py:113
  298.6 3.0 fusion.16
  301.6 8.3 %fusion.18 = bf16[512,2048]{1,0:T(8,128)(2,1)} fusion(bf16[1,1,768,2048]{3,2,1,0:T(8,128)(2,1)} %param.17, f32[512,768]{1,0:T(8,128)} %fusion.16, bf16[512,2048]{1,0:T(8,128)(2,1)} %bitcast.135, bf16[1,1,2048,768]{3,2,1,0:T(8,128)(2,1)S(1)} %copy-done), kind=kOutput, calls=%fused_computation.27 | convolution fusion | flops 3224633344 | bytes 12058624 | tf_op jit(solution)/shard_map/dot_general | solution.py:33
  309.9 5.2 %all-to-all-start.1 = ((bf16[32,16,2048]{2,1,0:T(8,128)(2,1)}), bf16[32,16,2048]{2,1,0:T(8,128)(2,1)}, u32[]{:S(2)}, u32[]{:S(2)}) async-start(bf16[32,16,2048]{2,1,0:T(8,128)(2,1)} %bitcast.133), calls=%async_computation.1 | async-start | bytes 4194304 | tf_op jit(solution)/shard_map/all_to_all | solution.py:121
  315.4 49.3 %all-to-all-done.1 = bf16[32,16,2048]{2,1,0:T(8,128)(2,1)} async-done(((bf16[32,16,2048]{2,1,0:T(8,128)(2,1)}), bf16[32,16,2048]{2,1,0:T(8,128)(2,1)}, u32[]{:S(2)}, u32[]{:S(2)}) %all-to-all-start.1) | async-done | bytes 2097184 | tf_op jit(solution)/shard_map/all_to_all | solution.py:121
  364.7 3.2 concatenate.6
  367.9 10.7 %gather_fusion.1 = bf16[1024,2048]{1,0:T(8,128)(2,1)} fusion(bf16[513,2048]{1,0:T(8,128)(2,1)} %concatenate.6, s32[1024]{0:T(1024)S(1)} %broadcast_clamp_fusion.1), kind=kCustom, calls=%fused_computation.1 | custom fusion | bytes 8392704 | tf_op jit(solution)/shard_map/gather | solution.py:70
  378.6 6.6 %fusion = f32[128,2048]{1,0:T(8,128)S(1)} fusion(bf16[1024,2048]{1,0:T(8,128)(2,1)} %gather_fusion.1, f32[128,8]{1,0:T(8,128)S(1)} %copy.27), kind=kLoop, calls=%fused_computation.7 | loop fusion | flops 6029312 | bytes 5246976 | tf_op jit(solution)/shard_map/reduce_sum | solution.py:124
  385.2 2.6 fusion.37
  (77 shorter events, 11.8 us)
Async XLA Ops:
  0.6 139.5 %copy-start = (bf16[1,1,2048,768]{3,2,1,0:T(8,128)(2,1)S(1)}, bf16[1,1,2048,768]{3,2,1,0:T(8,128)(2,1)}, u32[]{:S(2)}) copy-start(bf16[1,1,2048,768]{3,2,1,0:T(8,128)(2,1)} %param.16) | copy-start | bytes 9437188
  16.9 11.6 %copy-start.9 = (f32[1,128,8]{1,2,0:T(8,128)S(1)}, f32[1,128,8]{1,2,0:T(8,128)}, u32[]{:S(2)}) copy-start(f32[1,128,8]{1,2,0:T(8,128)} %param.21) | copy-start | bytes 12292
  16.9 61.6 %all-to-all-start.3 = ((bf16[32,16,2048]{2,1,0:T(8,128)(2,1)}), bf16[32,16,2048]{2,1,0:T(8,128)(2,1)}, u32[]{:S(2)}, u32[]{:S(2)}) async-start(bf16[32,16,2048]{2,1,0:T(8,128)(2,1)} %broadcast_select_fusion), calls=%async_computation.3 | async-start | bytes 4194304 | tf_op jit(solution)/shard_map/all_to_all | solution.py:114
  28.5 7.0 %collective-permute-start.1 = (bf16[1,128,2048]{2,1,0:T(8,128)(2,1)}, bf16[1,128,2048]{2,1,0:T(8,128)(2,1)}, u32[]{:S(2)}, u32[]{:S(2)}) collective-permute-start(bf16[1,128,2048]{2,1,0:T(8,128)(2,1)} %param.12), channel_id=1, source_target_pairs={{0,224},{32,0},{64,32},{96,64},{128,96},{160,128},{192,160},{224,1... | collective-permute-start | bytes 1572872 | tf_op jit(solution)/shard_map/ppermute | solution.py:14
  78.5 56.0 %all-to-all-start.2 = ((bf16[32,16,2048]{2,1,0:T(8,128)(2,1)}), bf16[32,16,2048]{2,1,0:T(8,128)(2,1)}, u32[]{:S(2)}, u32[]{:S(2)}) async-start(bf16[32,16,2048]{2,1,0:T(8,128)(2,1)} %fusion.1), calls=%async_computation.2 | async-start | bytes 4194304 | tf_op jit(solution)/shard_map/all_to_all | solution.py:115
  134.5 5.6 %copy-start.12 = (f32[512,768]{1,0:T(8,128)S(1)}, f32[512,768]{1,0:T(8,128)}, u32[]{:S(2)}) copy-start(f32[512,768]{1,0:T(8,128)} %fusion.14) | copy-start | bytes 4718596
  139.0 1.1 copy-start.13
  153.9 6.7 %copy-start.7 = (s32[1,128,8]{1,2,0:T(8,128)S(1)}, s32[1,128,8]{1,2,0:T(8,128)}, u32[]{:S(2)}) copy-start(s32[1,128,8]{1,2,0:T(8,128)} %param.19) | copy-start | bytes 12292
  153.9 6.9 %copy-start.8 = (s32[1,128,8]{1,2,0:T(8,128)S(1)}, s32[1,128,8]{1,2,0:T(8,128)}, u32[]{:S(2)}) copy-start(s32[1,128,8]{1,2,0:T(8,128)} %param.18) | copy-start | bytes 12292
  153.9 56.1 %all-to-all-start.4 = ((bf16[32,16,2048]{2,1,0:T(8,128)(2,1)}), bf16[32,16,2048]{2,1,0:T(8,128)(2,1)}, u32[]{:S(2)}, u32[]{:S(2)}) async-start(bf16[32,16,2048]{2,1,0:T(8,128)(2,1)} %bitcast.132), calls=%async_computation.4 | async-start | bytes 4194304 | tf_op jit(solution)/shard_map/all_to_all | solution.py:122
  160.5 8.9 %collective-permute-start = (bf16[1,128,2048]{2,1,0:T(8,128)(2,1)}, bf16[1,128,2048]{2,1,0:T(8,128)(2,1)}, u32[]{:S(2)}, u32[]{:S(2)}) collective-permute-start(bf16[1,128,2048]{2,1,0:T(8,128)(2,1)} %param.11), channel_id=1, source_target_pairs={{0,32},{32,64},{64,96},{96,128},{128,160},{160,192},{192,224},{224... | collective-permute-start | bytes 1572872 | tf_op jit(solution)/shard_map/ppermute | solution.py:14
  223.9 6.1 %copy-start.3 = (bf16[1,128,2048]{2,1,0:T(8,128)(2,1)S(1)}, bf16[1,128,2048]{2,1,0:T(8,128)(2,1)}, u32[]{:S(2)}) copy-start(bf16[1,128,2048]{2,1,0:T(8,128)(2,1)} %param.13) | copy-start | bytes 1572868
  223.9 6.1 %copy-start.6 = (f32[1,2048]{1,0:T(1,128)S(1)}, f32[1,2048]{1,0:T(1,128)}, u32[]{:S(2)}) copy-start(f32[1,2048]{1,0:T(1,128)} %param.14) | copy-start | bytes 24580
  229.0 1.0 copy-start.1
  240.3 58.3 %copy-start.11 = (bf16[1,1,2048,768]{3,2,1,0:T(8,128)(2,1)S(1)}, bf16[1,1,2048,768]{3,2,1,0:T(8,128)(2,1)}, u32[]{:S(2)}) copy-start(bf16[1,1,2048,768]{3,2,1,0:T(8,128)(2,1)} %param.15) | copy-start | bytes 9437188
  297.3 1.3 copy-start.5
  309.9 5.4 %copy-start.10 = (f32[1,128,8]{1,2,0:T(8,128)S(1)}, f32[1,128,8]{1,2,0:T(8,128)}, u32[]{:S(2)}) copy-start(f32[1,128,8]{1,2,0:T(8,128)} %param.20) | copy-start | bytes 12292
  309.9 54.8 %all-to-all-start.1 = ((bf16[32,16,2048]{2,1,0:T(8,128)(2,1)}), bf16[32,16,2048]{2,1,0:T(8,128)(2,1)}, u32[]{:S(2)}, u32[]{:S(2)}) async-start(bf16[32,16,2048]{2,1,0:T(8,128)(2,1)} %bitcast.133), calls=%async_computation.1 | async-start | bytes 4194304 | tf_op jit(solution)/shard_map/all_to_all | solution.py:121
  378.6 6.6 %copy-start.2 = (f32[128,2048]{1,0:T(8,128)S(1)}, f32[128,2048]{1,0:T(8,128)}, u32[]{:S(2)}) copy-start(f32[128,2048]{1,0:T(8,128)} %copy-done.1) | copy-start | bytes 3145732
  378.6 6.7 %copy-start.4 = (bf16[1,128,2048]{2,1,0:T(8,128)(2,1)S(1)}, bf16[1,128,2048]{2,1,0:T(8,128)(2,1)}, u32[]{:S(2)}) copy-start(bf16[1,128,2048]{2,1,0:T(8,128)(2,1)} %param.13) | copy-start | bytes 1572868
where the time goes:
time: 389 us; the launch traced here: 388 us
  waiting for transfers between devices  180 us (46%)
  blocking collectives  57 us (15%)
  local copies, waits for them, and re-layouts  51.7 us (13%)
  matrix products  35.1 us (9%)
  other arithmetic  33.7 us (9%)
  starting transfers between devices  29.8 us (8%)
    all_to_all x1, blocking collectives, local(): lax.all_to_all(send_fwd, 'expert', split_axis=0, concat_axis=0, tiled=True)  57 us
    all_to_all x1, waiting for transfers between devices, local(): lax.all_to_all(outputs, 'expert', split_axis=0, concat_axis=0, tiled=True)  49.3 us
    all_to_all x1, waiting for transfers between devices, local(): lax.all_to_all(send_cot, 'expert', split_axis=0, concat_axis=0, tiled=True)  44 us
    all_to_all x1, waiting for transfers between devices, local(): lax.all_to_all(grads, 'expert', split_axis=0, concat_axis=0, tiled=True)  39.3 us
    all_to_all x1, waiting for transfers between devices, local(): lax.all_to_all(send_rows, 'expert', split_axis=0, concat_axis=0, tiled=True)  33.4 us
    gather x2, local copies, waits for them, and re-layouts, gather_back(): return padded[slot]  21.4 us
    dot_general x3, matrix products, transposed(): lax.dot_general(left, right, (((1,), (1,)), ((), ())), preferred_element_...  18.2 us
    ppermute x2, waiting for transfers between devices, passed_along(): lax.ppermute(value, axis, [(i, (i + by) % peers) for i in range(peers)])  13.8 us
  transfers between devices with their start and end apart: 6, of which 6 were waited for; matrix products, arithmetic and copies ran while one was open for 5% of the time, Pallas kernels for 0%

commit v1 on v0

v1 whole, which is shorter than its diff:
```python
import functools

import jax
import jax.numpy as jnp
from jax import lax
from jax.experimental import pallas as pl
from jax.experimental.pallas import tpu as pltpu
from jax.sharding import PartitionSpec as P

EPS = 1e-06
MESH = pl.DeviceIdType.MESH
F32 = jnp.float32
BF16 = jnp.bfloat16

NX = 4
NZ = 8
SEC = 8
CAP = 16
TOK = 128
D = 2048
HID = 768
CLS = 4 * CAP
FULL = (128, 128, 128, 64)
ORDER = (0, 1, 7, 2, 6, 3, 5, 4)


def where_am_i():
    e = lax.axis_index("expert")
    return lax.axis_index("section"), e // NZ, e % NZ


def at(s, x, z):
    return (s, x * NZ + z)


def iota(shape, dim):
    return lax.broadcasted_iota(jnp.int32, shape, dim)


def one(cond):
    return jnp.where(cond, jnp.float32(1.0), jnp.float32(0.0))


def routing(picks, gates, x, z):
    tok = iota((TOK, TOK), 1)
    sub = iota((TOK, TOK), 0)
    weight = gates / jnp.sum(gates, axis=0, keepdims=True)
    lane_e = iota((32, TOK), 0)
    disp = lane_e // 4
    expert = ((x + lane_e % 4) % NX) * NZ + (z + disp) % NZ
    named = jnp.zeros((32, TOK), F32)
    share = jnp.zeros((32, TOK), F32)
    for j in range(picks.shape[0]):
        hit = picks[j : j + 1, :] == expert
        named = named + one(hit)
        share = share + jnp.where(hit, weight[j : j + 1, :], 0.0)
    place = jnp.dot(
        named.astype(BF16), one(sub < tok).astype(BF16), preferred_element_type=F32
    )
    dist = disp.astype(F32)
    up = jnp.max(named * jnp.where(disp < 4, dist, 0.0), axis=0, keepdims=True)
    down = jnp.max(named * jnp.where(disp > 4, 8.0 - dist, 0.0), axis=0, keepdims=True)
    far = jnp.max(jnp.where(disp == 4, named, 0.0), axis=0, keepdims=True)
    even = one(iota((1, TOK), 1) % 2 == 0)
    go_up = jnp.where(up == down, even, one(up > down))
    up = jnp.where(far * go_up > 0.0, 4.0, up)
    down = jnp.where(far * (1.0 - go_up) > 0.0, 4.0, down)

    def ranks(reach):
        row = jnp.broadcast_to(reach, (TOK, TOK))
        col = jnp.sum(jnp.where(sub == tok, row, 0.0), axis=1, keepdims=True)
        col = jnp.broadcast_to(col, (TOK, TOK))
        ahead = jnp.where(row > col, 1.0, jnp.where(row == col, one(tok < sub), 0.0))
        pos_col = jnp.sum(ahead, axis=1, keepdims=True)
        ahead = jnp.where(col > row, 1.0, jnp.where(row == col, one(sub < tok), 0.0))
        pos_row = jnp.sum(ahead, axis=0, keepdims=True)
        return pos_row, pos_col

    up_row, up_col = ranks(up)
    down_row, down_col = ranks(down)
    own = iota((1, TOK), 1).astype(F32)
    split = jnp.where(go_up > 0.0, up_row, down_row + 128.0)
    value = jnp.where(
        disp == 0, own, jnp.where(disp < 4, up_row, jnp.where(disp == 4, split, down_row))
    )
    slot = iota((32, CAP, TOK), 1).astype(F32)
    chosen = jnp.where(place[:, None, :] == slot, named[:, None, :], 0.0)
    index = jnp.sum(chosen * (value + 1.0)[:, None, :], axis=2, keepdims=True) - 1.0
    scale = jnp.sum(chosen * share[:, None, :], axis=2, keepdims=True)
    index = index.reshape(32 * CAP, 1)
    scale = scale.reshape(32 * CAP, 1)
    return index, scale, (up_row, down_row), (up_col, down_col), (up, down)


def prepare_kernel(
    caps,
    handoff,
    cotangent,
    picks_f,
    gates_f,
    picks_b,
    gates_b,
    arriving,
    upstream,
    meta,
    meta_t,
    pos,
    pos_t,
    flag,
    meta_send,
    flag_x,
    flag_s,
    big_send,
    big_recv,
    meta_ss,
    meta_rs,
    x_ss,
    x_rs,
    s_ss,
    s_rs,
):
    s, x, z = where_am_i()
    z_peer = lambda d: at(s, x, (z + d) % NZ)
    x_peer = lambda d: at(s, (x + d) % NX, z)
    s_peer = lambda d: at((s + d) % SEC, x, z)
    barrier = pltpu.get_barrier_semaphore()
    partners = (
        [z_peer(d) for d in range(1, NZ)]
        + [x_peer(d) for d in range(1, NX)]
        + [s_peer(d) for d in range(1, SEC)]
    )
    for peer in partners:
        pl.semaphore_signal(barrier, inc=1, device_id=peer, device_id_type=MESH)
    pl.semaphore_wait(barrier, len(partners))
    big = [
        pltpu.make_async_remote_copy(
            src, dst, big_send.at[i], big_recv.at[i], device_id=peer, device_id_type=MESH
        )
        for i, (src, dst, peer) in enumerate(
            ((handoff, arriving, s_peer(1)), (cotangent, upstream, s_peer(SEC - 1)))
        )
    ]
    for copy in big:
        copy.start()

    lane = iota((CLS, TOK), 1)
    table = jnp.zeros((CLS, TOK), F32)
    over = jnp.zeros((1, 1), F32)
    lane_t = iota((TOK, TOK), 1)
    columns = jnp.zeros((TOK, TOK), F32)
    for m, (picks, gates) in enumerate(((picks_f, gates_f), (picks_b, gates_b))):
        index, scale, rows, cols, reach = routing(picks[...], gates[...], x, z)
        for d in range(NZ):
            part = slice(d * CLS, (d + 1) * CLS)
            table = jnp.where(lane == 8 * d + 2 * m, index[part], table)
            table = jnp.where(lane == 8 * d + 2 * m + 1, scale[part], table)
        for i in range(2):
            pos[2 * m + i : 2 * m + i + 1, :] = rows[i]
            columns = jnp.where(lane_t == 2 * m + i, cols[i], columns)
            for k in range(4):
                count = jnp.sum(one(reach[i] > k + 0.5), axis=1, keepdims=True)
                over = jnp.maximum(over, one(count > caps[k] + 0.5))
    pos[4:8, :] = jnp.zeros((4, TOK), F32)
    pos_t[...] = columns
    whole = jnp.concatenate([table, jnp.zeros((CLS, TOK), F32)], axis=0)
    whole = jnp.transpose(whole)[:CLS, :]
    whole = jnp.where(iota((CLS, TOK), 0) % 8 == 4, jnp.broadcast_to(over, (CLS, TOK)), whole)
    meta_send[...] = whole
    meta[0:8, :] = whole[0:8, :]
    copies = []
    for d in range(1, NZ):
        part = pl.ds(8 * d, 8)
        copy = pltpu.make_async_remote_copy(
            meta_send.at[part],
            meta.at[part],
            meta_ss.at[d],
            meta_rs.at[d],
            device_id=z_peer(d),
            device_id_type=MESH,
        )
        copy.start()
        copies.append(copy)
    for copy in copies:
        copy.wait()
    got = meta[...]
    meta_t[...] = jnp.transpose(jnp.concatenate([got, jnp.zeros((CLS, TOK), F32)], axis=0))
    over = jnp.max(
        jnp.where(iota((CLS, TOK), 0) % 8 == 4, got, 0.0), axis=0, keepdims=True
    )

    def spread(over, buf, peers, send, recv):
        buf[0] = jnp.broadcast_to(over, (8, TOK))
        copies = []
        for d, peer in enumerate(peers, 1):
            copy = pltpu.make_async_remote_copy(
                buf.at[0],
                buf.at[d],
                send.at[d],
                recv.at[d],
                device_id=peer,
                device_id_type=MESH,
            )
            copy.start()
            copies.append(copy)
        for copy in copies:
            copy.wait()
        return jnp.max(jnp.max(buf[...], axis=0), axis=0, keepdims=True)

    over = spread(over, flag_x, [x_peer(d) for d in range(1, NX)], x_ss, x_rs)
    over = spread(over, flag_s, [s_peer(d) for d in range(1, SEC)], s_ss, s_rs)
    flag[...] = jnp.broadcast_to(over, (8, TOK))
    for copy in big:
        copy.wait()


def prepare(caps, handoff, cotangent, picks_f, gates_f, picks_b, gates_b):
    vmem = pl.BlockSpec(memory_space=pltpu.VMEM)
    hbm = pl.BlockSpec(memory_space=pl.ANY)
    rows = jax.ShapeDtypeStruct((TOK, D), BF16)
    sem = pltpu.SemaphoreType.DMA
    return pl.pallas_call(
        functools.partial(prepare_kernel, caps),
        out_shape=(
            rows,
            rows,
            jax.ShapeDtypeStruct((CLS, TOK), F32),
            jax.ShapeDtypeStruct((TOK, TOK), F32),
            jax.ShapeDtypeStruct((8, TOK), F32),
            jax.ShapeDtypeStruct((TOK, TOK), F32),
            jax.ShapeDtypeStruct((8, TOK), F32),
        ),
        in_specs=[hbm, hbm, vmem, vmem, vmem, vmem],
        out_specs=(hbm, hbm, vmem, vmem, vmem, vmem, vmem),
        scratch_shapes=[
            pltpu.VMEM((CLS, TOK), F32),
            pltpu.VMEM((NX, 8, TOK), F32),
            pltpu.VMEM((SEC, 8, TOK), F32),
            sem((2,)),
            sem((2,)),
            sem((NZ,)),
            sem((NZ,)),
            sem((NX,)),
            sem((NX,)),
            sem((SEC,)),
            sem((SEC,)),
        ],
        name="prepare",
        compiler_params=pltpu.CompilerParams(collective_id=0, has_side_effects=True),
    )(handoff, cotangent, picks_f, gates_f, picks_b, gates_b)


R_, C_, F_ = 0, 1, 2
G_, O_ = 0, 1


def layer_kernel(
    caps,
    saved,
    arriving,
    upstream,
    gain,
    meta,
    meta_t,
    pos,
    pos_t,
    w_gate,
    w_up,
    w_down,
    act,
    grad,
    wg,
    wu,
    wd,
    first,
    zbuf,
    xs,
    xr,
    yr,
    sb,
    rb,
    hid,
    scale_ref,
    w_sem,
    z_ss,
    z_rs,
    x_ss,
    x_rs,
    y_ss,
    y_rs,
    r_ss,
    r_rs,
):
    s, x, z = where_am_i()
    z_peer = lambda d: at(s, x, (z + d + NZ) % NZ)
    x_peer = lambda d: at(s, (x + d + NX) % NX, z)
    offs = [sum(caps[:k]) for k in range(5)]
    weights = [
        pltpu.make_async_copy(src, dst, w_sem.at[i])
        for i, (src, dst) in enumerate(((w_gate, wg), (w_up, wu), (w_down, wd)))
    ]
    for copy in weights:
        copy.start()
    barrier = pltpu.get_barrier_semaphore()
    partners = [z_peer(1), z_peer(-1), x_peer(1), x_peer(2), x_peer(3)]
    for peer in partners:
        pl.semaphore_signal(barrier, inc=1, device_id=peer, device_id_type=MESH)
    pl.semaphore_wait(barrier, len(partners))

    sends = []

    def remote(src, dst, send, recv, peer):
        copy = pltpu.make_async_remote_copy(
            src, dst, send, recv, device_id=peer, device_id_type=MESH
        )
        copy.start()
        sends.append(copy)
        return copy

    def normalize(ref):
        values = ref[...].astype(F32)
        scale = lax.rsqrt(jnp.mean(values * values, axis=-1, keepdims=True) + EPS)
        return (values * scale * gain[...]).astype(BF16), scale

    hops = {}

    def hop(stream, k):
        for way in range(2):
            part = pl.ds(offs[k - 1], caps[k - 1])
            if k == 1:
                src = first.at[stream, way, pl.ds(0, caps[0])]
            else:
                src = zbuf.at[stream, way, pl.ds(offs[k - 2], caps[k - 1])]
            hops[stream, way, k] = remote(
                src,
                zbuf.at[stream, way, part],
                z_ss.at[stream, way, k - 1],
                z_rs.at[stream, way, k - 1],
                z_peer(1 - 2 * way),
            )

    def sort_rows(stream, rows):
        m = 0 if stream == F_ else 1
        for way in range(2):
            order = pos[2 * m + way : 2 * m + way + 1, :]
            perm = one(order == iota((TOK, TOK), 0).astype(F32)).astype(BF16)
            first[stream, way] = jnp.dot(perm, rows, preferred_element_type=F32).astype(BF16)

    xcopies = {}

    def gather(stream, d, rows):
        m = 0 if stream == F_ else 1
        index = meta_t[0:CLS, 8 * d + 2 * m : 8 * d + 2 * m + 1]
        total = None
        for values, base in rows:
            n = values.shape[0]
            sel = one(index == (iota((CLS, n), 1) + base).astype(F32)).astype(BF16)
            part = jnp.dot(sel, values, preferred_element_type=F32)
            total = part if total is None else total + part
        if stream == C_:
            total = total * meta_t[0:CLS, 8 * d + 3 : 8 * d + 4]
        total = total.astype(BF16)
        base = ORDER.index(d) * CLS
        xr[stream, base : base + CAP, :] = total[0:CAP]
        xs[stream, base + CAP : base + CLS, :] = total[CAP:CLS]
        for o in range(1, NX):
            part = pl.ds(base + o * CAP, CAP)
            xcopies[stream, d, o] = remote(
                xs.at[stream, part],
                xr.at[stream, part],
                x_ss.at[stream, d, o],
                x_rs.at[stream, d, o],
                x_peer(o),
            )

    def ring_rows(stream, way, k):
        return zbuf[stream, way, offs[k - 1] : offs[k], :]

    def arrive(stream, k):
        for way in range(2):
            hops[stream, way, k].wait_recv()
        if k < 4:
            hop(stream, k + 1)
            gather(stream, k, [(ring_rows(stream, 0, k), 0)])
            gather(stream, NZ - k, [(ring_rows(stream, 1, k), 0)])
        else:
            gather(stream, 4, [(ring_rows(stream, 0, 4), 0), (ring_rows(stream, 1, 4), 128)])

    def slots_ready(stream, half):
        for d in ORDER[4 * half : 4 * half + 4]:
            for o in range(1, NX):
                xcopies[stream, d, o].wait_recv()

    HALF = 4 * CLS
    nt = lambda a, b: lax.dot_general(
        a, b, (((1,), (1,)), ((), ())), preferred_element_type=F32
    )
    nn = lambda a, b: jnp.dot(a, b, preferred_element_type=F32)
    ycopies = {}

    def keep(stream, src, half, cols, out):
        out = out.astype(BF16)
        xr[src, half * HALF : (half + 1) * HALF, cols] = out
        for p in range(4):
            base = half * HALF + p * CLS
            yr[stream, base : base + CAP, cols] = out[p * CLS : p * CLS + CAP]

    def send_back(stream, src, half):
        for d in reversed(ORDER[4 * half : 4 * half + 4]):
            base = ORDER.index(d) * CLS
            for o in range(1, NX):
                part = pl.ds(base + o * CAP, CAP)
                ycopies[stream, d, o] = remote(
                    xr.at[src, part],
                    yr.at[stream, part],
                    y_ss.at[stream, d, o],
                    y_rs.at[stream, d, o],
                    x_peer(-o),
                )

    def backward(half):
        rows = slice(half * HALF, (half + 1) * HALF)

        @pl.loop(0, HID // 256)
        def _(b):
            cols = pl.ds(pl.multiple_of(b * 256, 256), 256)
            gate_act = nn(xr[R_, rows, :], wg[:, cols])
            up_act = nn(xr[R_, rows, :], wu[:, cols])
            hid_grad = nt(xr[C_, rows, :], wd[cols, :])
            sigma = jax.nn.sigmoid(gate_act)
            hid[0, :, cols] = (
                hid_grad * up_act * sigma * (1.0 + gate_act * (1.0 - sigma))
            ).astype(BF16)
            hid[1, :, cols] = (hid_grad * gate_act * sigma).astype(BF16)

        @pl.loop(0, D // 256)
        def _(b):
            cols = pl.ds(pl.multiple_of(b * 256, 256), 256)
            keep(G_, R_, half, cols, nt(hid[0], wg[cols, :]) + nt(hid[1], wu[cols, :]))

        send_back(G_, R_, half)

    def forward(half):
        rows = slice(half * HALF, (half + 1) * HALF)

        @pl.loop(0, HID // 256)
        def _(b):
            cols = pl.ds(pl.multiple_of(b * 256, 256), 256)
            gate_act = nn(xr[F_, rows, :], wg[:, cols])
            up_act = nn(xr[F_, rows, :], wu[:, cols])
            hid[0, :, cols] = (jax.nn.silu(gate_act) * up_act).astype(BF16)

        @pl.loop(0, D // 256)
        def _(b):
            cols = pl.ds(pl.multiple_of(b * 256, 256), 256)
            keep(O_, F_, half, cols, nn(hid[0], wd[:, cols]))

        send_back(O_, F_, half)

    def class_rows(stream, d, n, base):
        for o in range(1, NX):
            if (stream, d, o) in ycopies:
                ycopies.pop((stream, d, o)).wait_recv()
        m = 0 if stream == O_ else 1
        start = ORDER.index(d) * CLS
        values = yr[stream, start : start + CLS, :]
        if stream == O_:
            values = (values.astype(F32) * meta_t[0:CLS, 8 * d + 1 : 8 * d + 2]).astype(BF16)
        index = meta[8 * d + 2 * m : 8 * d + 2 * m + 1, 0:CLS]
        sel = one(index == (iota((n, CLS), 0) + base).astype(F32)).astype(BF16)
        return jnp.dot(sel, values, preferred_element_type=F32)

    backs = {}

    def combine(stream, k):
        for way in range(2):
            n = caps[k - 1]
            d = k if way == 0 else NZ - k
            total = class_rows(stream, d, n, 128 * way if k == 4 else 0)
            part = slice(offs[k - 1], offs[k])
            if k < 4:
                backs[stream, way, k + 1].wait_recv()
                more = caps[k]
                near = rb[stream, way, offs[k] : offs[k + 1], :].astype(F32)
                head = (total[:more] + near).astype(BF16)
                sb[stream, way, offs[k - 1] : offs[k - 1] + more, :] = head
                if more < n:
                    sb[stream, way, offs[k - 1] + more : offs[k], :] = total[more:].astype(BF16)
            else:
                sb[stream, way, part, :] = total.astype(BF16)
            part = pl.ds(offs[k - 1], n)
            backs[stream, way, k] = remote(
                sb.at[stream, way, part],
                rb.at[stream, way, part],
                r_ss.at[stream, way, k - 1],
                r_rs.at[stream, way, k - 1],
                z_peer(2 * way - 1),
            )

    def home(stream):
        m = 0 if stream == O_ else 1
        total = class_rows(stream, 0, TOK, 0)
        for way in range(2):
            backs[stream, way, 1].wait_recv()
            col = pos_t[:, 2 * m + way : 2 * m + way + 1]
            sel = one(col == iota((TOK, caps[0]), 1).astype(F32)).astype(BF16)
            total = total + jnp.dot(
                sel, rb[stream, way, 0 : caps[0], :], preferred_element_type=F32
            )
        return total

    rows, scale = normalize(saved)
    scale_ref[...] = scale
    sort_rows(R_, rows)
    hop(R_, 1)
    gather(R_, 0, [(rows, 0)])
    sort_rows(C_, upstream[...])
    hop(C_, 1)
    gather(C_, 0, [(upstream[...], 0)])
    rows, unused = normalize(arriving)
    sort_rows(F_, rows)
    gather(F_, 0, [(rows, 0)])
    arrive(R_, 1)
    arrive(C_, 1)
    hop(F_, 1)
    arrive(R_, 2)
    arrive(C_, 2)
    arrive(F_, 1)
    arrive(R_, 3)
    arrive(C_, 3)
    arrive(F_, 2)
    arrive(R_, 4)
    arrive(C_, 4)
    for copy in weights:
        copy.wait()
    slots_ready(R_, 0)
    slots_ready(C_, 0)
    backward(0)
    arrive(F_, 3)
    slots_ready(R_, 1)
    slots_ready(C_, 1)
    backward(1)
    arrive(F_, 4)
    combine(G_, 4)
    slots_ready(F_, 0)
    forward(0)
    combine(G_, 3)
    slots_ready(F_, 1)
    forward(1)
    combine(G_, 2)
    combine(O_, 4)
    combine(G_, 1)
    combine(O_, 3)
    total = home(G_)
    gained = gain[...] * total
    values = saved[...].astype(F32)
    scale = scale_ref[...]
    cube = scale * scale * scale
    grad[...] = (
        upstream[...].astype(F32)
        + scale * gained
        - values * cube * jnp.mean(values * gained, axis=1, keepdims=True)
    ).astype(BF16)
    combine(O_, 2)
    combine(O_, 1)
    act[...] = (arriving[...].astype(F32) + home(O_)).astype(BF16)
    for copy in sends:
        copy.wait_send()


def layer(caps, cid, *args):
    vmem = pl.BlockSpec(memory_space=pltpu.VMEM)
    hbm = pl.BlockSpec(memory_space=pl.ANY)
    rows = jax.ShapeDtypeStruct((TOK, D), BF16)
    sem = pltpu.SemaphoreType.DMA
    total = sum(caps)
    slots = NZ * CLS
    return pl.pallas_call(
        functools.partial(layer_kernel, caps),
        out_shape=(rows, rows),
        in_specs=[vmem] * 8 + [hbm] * 3,
        out_specs=(vmem, vmem),
        scratch_shapes=[
            pltpu.VMEM((D, HID), BF16),
            pltpu.VMEM((D, HID), BF16),
            pltpu.VMEM((HID, D), BF16),
            pltpu.VMEM((3, 2, TOK, D), BF16),
            pltpu.VMEM((3, 2, total, D), BF16),
            pltpu.VMEM((3, slots, D), BF16),
            pltpu.VMEM((3, slots, D), BF16),
            pltpu.VMEM((2, slots, D), BF16),
            pltpu.VMEM((2, 2, total, D), BF16),
            pltpu.VMEM((2, 2, total, D), BF16),
            pltpu.VMEM((2, 4 * CLS, HID), BF16),
            pltpu.VMEM((TOK, 1), F32),
            sem((3,)),
            sem((3, 2, 4)),
            sem((3, 2, 4)),
            sem((3, NZ, NX)),
            sem((3, NZ, NX)),
            sem((2, NZ, NX)),
            sem((2, NZ, NX)),
            sem((2, 2, 4)),
            sem((2, 2, 4)),
        ],
        name="layer%d" % cid,
        compiler_params=pltpu.CompilerParams(
            collective_id=cid, has_side_effects=True, vmem_limit_bytes=67043328
        ),
    )(*args)


def local(
    handoff,
    cotangent_handoff,
    saved_input,
    norm_gain,
    w_gate,
    w_up,
    w_down,
    picks_fwd,
    picks_bwd,
    gates_fwd,
    gates_bwd,
):
    caps = FULL
    arriving, upstream, meta, meta_t, pos, pos_t, flag = prepare(
        caps,
        handoff[0],
        cotangent_handoff[0],
        picks_fwd[0].T,
        gates_fwd[0].T,
        picks_bwd[0].T,
        gates_bwd[0].T,
    )
    args = (
        saved_input[0],
        arriving,
        upstream,
        norm_gain,
        meta,
        meta_t,
        pos,
        pos_t,
        w_gate[0, 0],
        w_up[0, 0],
        w_down[0, 0],
    )
    act, grad = layer(FULL, 1, *args)
    return (act[None], grad[None])


def solution(mesh):
    in_specs = (
        P("section", "expert", None),
        P("section", "expert", None),
        P("section", "expert", None),
        P("section", None),
        P("section", "expert", None, None),
        P("section", "expert", None, None),
        P("section", "expert", None, None),
        P("section", "expert", None),
        P("section", "expert", None),
        P("section", "expert", None),
        P("section", "expert", None),
    )
    out_specs = (P("section", "expert", None), P("section", "expert", None))
    return jax.shard_map(local, mesh=mesh, in_specs=in_specs, out_specs=out_specs, check_vma=False)
```

time: 389 us -> 254 us (0.65)
  Pallas kernels: 0 us -> 247 us
  waiting for transfers between devices: 180 us -> 0 us
  blocking collectives: 57 us -> 0 us
  local copies, waits for them, and re-layouts: 51.7 us -> 3.76 us
  matrix products: 35.1 us -> 0 us
  other arithmetic: 33.7 us -> 0 us
  starting transfers between devices: 29.8 us -> 0 us
    pallas_call x0 -> x2, Pallas kernels: none -> 247 us  [the longest x1 225 us: layer(): pl.pallas_call(functools.partial(layer_kernel, caps), out_shape=(rows, ro...]
    all_to_all x4 -> x0, waiting for transfers between devices: 166 us -> none  [the longest x1 49.3 us: local(): lax.all_to_all(outputs, 'expert', split_axis=0, concat_axis=0, tiled=True)]
    all_to_all x1 -> x0, blocking collectives: 57 us -> none  [local(): lax.all_to_all(send_fwd, 'expert', split_axis=0, concat_axis=0, tiled=True)]
    gather x5 -> x0, local copies, waits for them, and re-layouts: 40.5 us -> none  [the longest x2 21.4 us: gather_back(): return padded[slot]]
    dot_general x6 -> x0, matrix products: 35.1 us -> none  [the longest x3 18.2 us: transposed(): lax.dot_general(left, right, (((1,), (1,)), ((), ())), preferred_element_...]
    all_to_all x4 -> x0, starting transfers between devices: 29.8 us -> none  [the longest x1 11.6 us: local(): lax.all_to_all(send_rows, 'expert', split_axis=0, concat_axis=0, tiled=True)]
    reduce_sum x14 -> x0, other arithmetic: 18.9 us -> none  [the longest x1 6.63 us: local(): mixed = jnp.sum(weight_f[:, :, None] * picked, axis=1)]
    ppermute x2 -> x0, waiting for transfers between devices: 13.8 us -> none  [passed_along(): lax.ppermute(value, axis, [(i, (i + by) % peers) for i in range(peers)])]
  transfers between devices with their start and end apart: 6 -> 0, of which waited for: 6 -> 0; matrix products, arithmetic and copies ran while one was open for 5% -> 0% of each run, Pallas kernels for 0% -> 0%
where the time goes in v1:
time: 254 us; the launch traced here: 252 us
  Pallas kernels  247 us (97%)
  local copies, waits for them, and re-layouts  3.76 us (1%)
    pallas_call x1, Pallas kernels, layer(): pl.pallas_call(functools.partial(layer_kernel, caps), out_shape=(rows, ro...  225 us
    pallas_call x1, Pallas kernels, prepare(): pl.pallas_call(functools.partial(prepare_kernel, caps), out_shape=(rows,...  22.3 us

profile of v1, /device:TPU:8, one launch (start us, length us, event | category | flops | bytes accessed | tf_op | source)
XLA Modules:
  0.0 251.8 jit_solution(6247799725128961799)
XLA Ops:
  0.6 22.3 %prepare.1 = (bf16[128,2048]{1,0:T(8,128)(2,1)}, bf16[128,2048]{1,0:T(8,128)(2,1)}, f32[64,128]{1,0:T(8,128)}, f32[128,128]{1,0:T(8,128)}, f32[8,128]{1,0:T(8,12...) custom-call(bf16[128,2048]{1,0:T(8,128)(2,1)} %bitcast.24, bf16[128,2048]{1,0:T(8,128)(2,1)} %bitcast.25, s32[8,128]{1,0:T(8,128)} %bitcast.28, ...), custom_call_target="tpu_custom_call" | custom-call | tf_op jit(solution)/shard_map/prepare/pallas_call | solution.py:221
  22.9 225.1 %layer1.1 = (bf16[128,2048]{1,0:T(8,128)(2,1)}, bf16[128,2048]{1,0:T(8,128)(2,1)}) custom-call(bf16[128,2048]{1,0:T(8,128)(2,1)} %bitcast.23, bf16[128,2048]{1,0:T(8,128)(2,1)} %get-tuple-element.10.arriving, bf16[128,2048]{1,0:T(8,128)(2,1)} %get-tuple-element.11.upstream, f32[1,2048]{1,0:T(1,128)} %gain.1, f32[64,128]{1,0:T(8,128)} %get-tuple-element.12.meta, ...), custom_call_target="tpu_custom_call" | custom-call | tf_op jit(solution)/shard_map/layer1/pallas_call | solution.py:577
  248.1 1.9 copy.15
  250.0 1.9 copy.16
